TPU v7x, 32 devices: a whole 2x2x4 slice. The times are simulated.
32 devices in a mesh: head: 4 (over y, x), seq: 8 (over z, core).
Axes of the slice: x: 2, y: 2, z: 4, core: 2. Of those that a mesh axis runs over, the one named last changes fastest.
Arguments:
- queries: bfloat16 [4096, 8192], P('seq', 'head'), may hold values from -200 to 200
- keys: bfloat16 [4096, 8192], P('seq', 'head'), may hold values from -6 to 6
- values: bfloat16 [4096, 8192], P('seq', 'head'), may hold values from -6 to 6
- cotangent: bfloat16 [4096, 8192], P('seq', 'head'), may hold values from -6 to 6
- prefix_keys: bfloat16 [4096, 8192], P('seq', 'head'), may hold values from -1.5 to 1.5
- prefix_values: bfloat16 [4096, 8192], P('seq', 'head'), may hold values from -1.5 to 1.5
- gain: float32 [8192], P('head'), may hold values from 0.5 to 1.5
- lengths: int32 [8], P('seq'), may hold values from 64 to 512, as said below
Outputs:
- normed: bfloat16 [4096, 8192], P('seq', 'head')
- query_grad: bfloat16 [4096, 8192], P('seq', 'head')
- key_grad: bfloat16 [4096, 8192], P('seq', 'head')
- value_grad: bfloat16 [4096, 8192], P('seq', 'head')
- prefix_key_grad: bfloat16 [4096, 8192], P('seq', 'head')
- prefix_value_grad: bfloat16 [4096, 8192], P('seq', 'head')
Inputs may be any that keep to these rules, and one draw needn't show every extreme that they name: `lengths`: one length per response; some response has exactly 512 live slots and some exactly 64.
All inputs are finite; a program needn't handle non-finite values.
Results may differ from a plain program's by a relative error of at most 0.0058.
Values sent between devices are 32-bit elements; how exact they have to be, the bound alone decides.
A program may use at most 128 MiB of HBM per device.

v0:
```python
import functools

import jax
import jax.numpy as jnp
from jax import lax
from jax.sharding import PartitionSpec as P

H = 64
HEAD_DIM = 128
BLOCK = 256


epsilon = 1e-06


def summed_prefix(partial_state):
    return lax.psum(partial_state, "seq")


def body(queries, keys, values, cotangent, prefix_keys, prefix_values, gain, lengths):
    tok_rows, tok_cols = queries.shape
    heads_here = tok_cols // HEAD_DIM
    block_count = tok_rows // BLOCK
    length = lengths[0]
    is_live = lax.iota(jnp.int32, tok_rows) < length
    live_mask = is_live.astype(jnp.bfloat16)[:, None]
    block_shape = (block_count, BLOCK, heads_here, HEAD_DIM)
    q_live = (queries * live_mask).reshape(block_shape)
    k_live = (keys * live_mask).reshape(block_shape)
    v_live = (values * live_mask).reshape(block_shape)
    causal = (lax.iota(jnp.int32, BLOCK)[:, None] >= lax.iota(jnp.int32, BLOCK)[None, :]).astype(
        jnp.float32
    )
    pre_keys = prefix_keys.reshape(-1, heads_here, HEAD_DIM)
    pre_values = prefix_values.reshape(-1, heads_here, HEAD_DIM)
    partial_state = jnp.einsum(
        "thd,the->hde", pre_keys, pre_values, preferred_element_type=jnp.float32
    )

    def intra_block(index):
        q_block = q_live[index]
        k_block = k_live[index]
        v_block = v_live[index]
        scores = jnp.einsum("bhd,shd->hbs", q_block, k_block, preferred_element_type=jnp.float32)
        scores = (scores * causal).astype(jnp.bfloat16)
        in_block = jnp.einsum("hbs,she->bhe", scores, v_block, preferred_element_type=jnp.float32)
        block_kv = jnp.einsum("bhd,bhe->hde", k_block, v_block, preferred_element_type=jnp.float32)
        return (in_block, scores, block_kv)

    def from_state_of(index, state_bf):
        return jnp.einsum(
            "bhd,hde->bhe", q_live[index], state_bf, preferred_element_type=jnp.float32
        )

    results = []
    score_list = []
    state_list = []
    prefix_state = summed_prefix(partial_state)

    def forward_block(index, state_now):
        state_bf = state_now.astype(jnp.bfloat16)
        in_block, scores, block_kv = intra_block(index)
        return (from_state_of(index, state_bf) + in_block, scores, state_bf, state_now + block_kv)

    state_now = prefix_state
    for index in range(block_count):
        step_fn = functools.partial(forward_block, index)
        packed = step_fn(state_now)
        results.append(packed[0])
        score_list.append(packed[1])
        state_list.append(packed[2])
        state_now = packed[3]
    attended = jnp.concatenate(results, axis=0).reshape(tok_rows, tok_cols)
    scaled_cot = gain * (cotangent * live_mask).astype(jnp.float32)
    square_sum, inner_sum = lax.psum(
        (jnp.sum(attended * attended, axis=1), jnp.sum(scaled_cot * attended, axis=1)), "head"
    )
    root_mean = jnp.sqrt(square_sum / (H * HEAD_DIM) + epsilon)[:, None]
    inner_sum = inner_sum[:, None]
    normed = (gain * attended / root_mean).astype(jnp.bfloat16)
    out_grad = scaled_cot / root_mean - attended * inner_sum / (H * HEAD_DIM * root_mean**3)
    out_grad = out_grad.astype(jnp.bfloat16).reshape(block_shape)

    def backward_block(index, grad_state):
        q_block = q_live[index]
        k_block = k_live[index]
        v_block = v_live[index]
        d_block = out_grad[index]
        scores = score_list[index]
        state_bf = state_list[index]
        grad_bf = grad_state.astype(jnp.bfloat16)
        pscore = jnp.einsum("bhe,she->hbs", d_block, v_block, preferred_element_type=jnp.float32)
        pscore = (pscore * causal).astype(jnp.bfloat16)
        grad_q = jnp.einsum(
            "bhe,hde->bhd", d_block, state_bf, preferred_element_type=jnp.float32
        ) + jnp.einsum("hbs,shd->bhd", pscore, k_block, preferred_element_type=jnp.float32)
        grad_k = jnp.einsum(
            "bhe,hde->bhd", v_block, grad_bf, preferred_element_type=jnp.float32
        ) + jnp.einsum("hbs,bhd->shd", pscore, q_block, preferred_element_type=jnp.float32)
        grad_v = jnp.einsum(
            "bhd,hde->bhe", k_block, grad_bf, preferred_element_type=jnp.float32
        ) + jnp.einsum("hbs,bhe->she", scores, d_block, preferred_element_type=jnp.float32)
        grad_next = grad_state + jnp.einsum(
            "bhd,bhe->hde", q_block, d_block, preferred_element_type=jnp.float32
        )
        return (
            grad_q.astype(jnp.bfloat16),
            grad_k.astype(jnp.bfloat16),
            grad_v.astype(jnp.bfloat16),
            grad_next,
        )

    grad_state = jnp.zeros((heads_here, HEAD_DIM, HEAD_DIM), jnp.float32)
    query_parts = []
    key_parts = []
    value_parts = []
    for index in reversed(range(block_count)):
        step_fn = functools.partial(backward_block, index)
        packed = step_fn(grad_state)
        query_parts.insert(0, packed[0])
        key_parts.insert(0, packed[1])
        value_parts.insert(0, packed[2])
        grad_state = packed[3]
    total_grad = lax.psum(grad_state, "seq")
    wide_keys = pre_keys.astype(jnp.float32)
    wide_values = pre_values.astype(jnp.float32)
    prefix_key_grad = jnp.einsum(
        "the,hde->thd", wide_values, total_grad, precision=lax.Precision.HIGHEST
    )
    prefix_value_grad = jnp.einsum(
        "thd,hde->the", wide_keys, total_grad, precision=lax.Precision.HIGHEST
    )
    query_grad = jnp.concatenate(query_parts, axis=0).reshape(tok_rows, tok_cols)
    key_grad = jnp.concatenate(key_parts, axis=0).reshape(tok_rows, tok_cols)
    value_grad = jnp.concatenate(value_parts, axis=0).reshape(tok_rows, tok_cols)
    return (
        normed,
        query_grad,
        key_grad,
        value_grad,
        prefix_key_grad.astype(jnp.bfloat16).reshape(prefix_keys.shape),
        prefix_value_grad.astype(jnp.bfloat16).reshape(prefix_values.shape),
    )


def solution(mesh):
    return jax.shard_map(
        body,
        mesh=mesh,
        in_specs=(
            P("seq", "head"),
            P("seq", "head"),
            P("seq", "head"),
            P("seq", "head"),
            P("seq", "head"),
            P("seq", "head"),
            P("head"),
            P("seq"),
        ),
        out_specs=(
            P("seq", "head"),
            P("seq", "head"),
            P("seq", "head"),
            P("seq", "head"),
            P("seq", "head"),
            P("seq", "head"),
        ),
        check_vma=False,
    )
```

profile of v0, /device:TPU:0, one launch (start us, length us, event | category | flops | bytes accessed | tf_op | source)
XLA Modules:
  0.0 200.3 jit_solution(2476563239131494849)
XLA Ops:
  8.8 3.4 %fusion.8 = f32[16,128,128]{2,1,0:T(8,128)} fusion(bf16[512,2048]{1,0:T(8,128)(2,1)} %param.13, bf16[512,2048]{1,0:T(8,128)(2,1)S(1)} %copy-done), kind=kOutput, calls=%fused_computation.18 | convolution fusion | flops 268435456 | bytes 5242880 | tf_op jit(solution)/shard_map/thd,the->hde/dot_general | solution.py:36
  13.0 3.9 %copy.49 = bf16[512,2048]{0,1:T(8,128)(2,1)} copy(bf16[512,2048]{1,0:T(8,128)(2,1)} %param.8) | data formatting | bytes 4194304 | tf_op args[0]
  16.9 3.9 %copy.53 = bf16[512,2048]{0,1:T(8,128)(2,1)} copy(bf16[512,2048]{1,0:T(8,128)(2,1)} %param.9) | data formatting | bytes 4194304 | tf_op args[1]
  20.8 3.9 %copy.52 = bf16[512,2048]{0,1:T(8,128)(2,1)} copy(bf16[512,2048]{1,0:T(8,128)(2,1)} %param.10) | data formatting | bytes 4194304 | tf_op args[2]
  24.7 3.3 %broadcast_multiply_fusion = (bf16[512,2048]{0,1:T(8,128)(2,1)S(1)}, bf16[512,2048]{0,1:T(8,128)(2,1)S(1)}, bf16[512,2048]{0,1:T(8,128)(2,1)S(1)}) fusion(bf16[512,2048]{0,1:T(8,128)(2,1)} %copy.53, bf16[512]{0:T(512)(128)(2,1)S(1)} %fusion.38, bf16[512,2048]{0,1:T(8,128)(2,1)} %copy.52, bf16[512,2048]{0,1:T(8,128)(2,1)} %copy.49), kind=kLoop, calls=%fused_computation.49 | loop fusion | flops 3145728 | bytes 12583936 | tf_op jit(solution)/shard_map/mul | solution.py:29
  30.9 2.1 %fusion.45 = f32[16,128,256]{2,1,0:T(8,128)} fusion(bf16[256,16,128]{0,2,1:T(8,128)(2,1)S(1)} %bitcast.125, bf16[16,256,256]{2,1,0:T(8,128)(2,1)S(1)} %multiply_convert_fusion.3), kind=kOutput, calls=%fused_computation.71 | convolution fusion | flops 268435456 | bytes 5242880 | tf_op jit(solution)/shard_map/hbs,she->bhe/dot_general | solution.py:46
  35.1 3.9 %copy.61 = bf16[512,2048]{0,1:T(8,128)(2,1)} copy(bf16[512,2048]{1,0:T(8,128)(2,1)} %param.11) | data formatting | bytes 4194304 | tf_op args[3]
  39.0 4.1 %fusion.46 = f32[16,128,256]{2,1,0:T(8,128)} fusion(bf16[256,16,128]{0,2,1:T(8,128)(2,1)} %bitcast.148, bf16[16,256,256]{2,1,0:T(8,128)(2,1)} %multiply_convert_fusion.2), kind=kOutput, calls=%fused_computation.72 | convolution fusion | flops 268435456 | bytes 5242880 | tf_op jit(solution)/shard_map/hbs,she->bhe/dot_general | solution.py:46
  43.1 31.3 %all-reduce.4.cloned.1.call-done = f32[16,128,128]{2,1,0:T(8,128)} async-done(((f32[16,128,128]{2,1,0:T(8,128)}), f32[16,128,128]{2,1,0:T(8,128)}) %all-reduce.4.cloned.1.call-update) | async-done | bytes 1048592 | tf_op jit(solution)/shard_map/psum | solution.py:17
  82.4 9.9 %all-reduce = (f32[512]{0:T(512)S(1)}, f32[512]{0:T(512)S(1)}) all-reduce(f32[512]{0:T(512)S(1)} %get-tuple-element.22, f32[512]{0:T(512)S(1)} %fusion.2), channel_id=1, replica_groups=mesh['head'=4,'seq'=8] {'head'}, use_global_device_ids=true, to_apply=%region_2.0 | all-reduce | flops 1024 | bytes 8192 | tf_op jit(solution)/shard_map/psum | solution.py:75
  92.3 4.5 %fusion.5 = (bf16[512,2048]{0,1:T(8,128)(2,1)S(1)}, bf16[512,2048]{0,1:T(8,128)(2,1)}) fusion(f32[512,16,128]{0,2,1:T(8,128)} %copy-done.1, f32[512]{0:T(512)S(1)} %get-tuple-element.32, f32[512]{0:T(512)S(1)} %get-tuple-element.19, f32[512]{0:T(512)S(1)} %get-tuple-element.33, f32[2048]{0:T(1024)S(1)} %copy-done.35, bf16[512,2048]{0,1:T(8,128)(2,1)} %copy.61, ...), kind=kLoop, calls=%fused_computation.9 | loop fusion | flops 11534336 | bytes 10501120 | tf_op jit(solution)/shard_map/convert_element_type | solution.py:82
  97.0 2.2 %copy-done.18 = bf16[16,256,256]{2,1,0:T(8,128)(2,1)S(1)} copy-done((bf16[16,256,256]{2,1,0:T(8,128)(2,1)S(1)}, bf16[16,256,256]{2,1,0:T(8,128)(2,1)}, u32[]{:S(2)}) %copy-start.18) | copy-done | bytes 2097176
  116.1 3.4 %fusion.27 = bf16[256,16,128]{0,2,1:T(8,128)(2,1)} fusion(f32[16,128,256]{2,1,0:T(8,128)} %fusion.52, bf16[256,16,128]{0,2,1:T(8,128)(2,1)S(1)} %bitcast.124, f32[16,128,128]{2,1,0:T(8,128)} %copy-done.19), kind=kOutput, calls=%fused_computation.44 | convolution fusion | flops 135528448 | bytes 5242880 | tf_op jit(solution)/shard_map/bhd,hde->bhe/dot_general | solution.py:100
  119.5 3.6 %fusion.26 = bf16[256,16,128]{0,2,1:T(8,128)(2,1)} fusion(f32[16,128,256]{2,1,0:T(8,128)} %fusion.51, bf16[256,16,128]{0,2,1:T(8,128)(2,1)} %bitcast.149), kind=kOutput, calls=%fused_computation.43 | convolution fusion | flops 135266304 | bytes 4194304 | tf_op jit(solution)/shard_map/bhe,hde->bhd/dot_general | solution.py:97
  129.6 3.9 %copy.82 = bf16[512,2048]{1,0:T(8,128)(2,1)} copy(bf16[512,2048]{0,1:T(8,128)(2,1)} %bitcast.151) | data formatting | bytes 4194304
  133.6 4.0 %copy.80 = bf16[512,2048]{1,0:T(8,128)(2,1)} copy(bf16[512,2048]{0,1:T(8,128)(2,1)} %bitcast.152) | data formatting | bytes 4194304
  137.6 2.4 %fusion.25 = bf16[256,16,128]{0,2,1:T(8,128)(2,1)S(1)} fusion(f32[16,128,256]{2,1,0:T(8,128)} %fusion.50, bf16[256,16,128]{0,2,1:T(8,128)(2,1)S(1)} %bitcast.128, f32[16,128,128]{2,1,0:T(8,128)} %copy-done.19), kind=kOutput, calls=%fused_computation.42 | convolution fusion | flops 135528448 | bytes 5242880 | tf_op jit(solution)/shard_map/bhe,hde->bhd/dot_general | solution.py:97
  141.5 3.9 %copy.81 = bf16[512,2048]{1,0:T(8,128)(2,1)} copy(bf16[512,2048]{0,1:T(8,128)(2,1)} %bitcast.153) | data formatting | bytes 4194304
  145.4 3.9 %copy.79 = bf16[512,2048]{1,0:T(8,128)(2,1)} copy(bf16[512,2048]{0,1:T(8,128)(2,1)} %get-tuple-element.21) | data formatting | bytes 4194304
  149.4 27.0 %all-reduce.6.cloned.1.call-done = f32[16,128,128]{2,1,0:T(8,128)} async-done(((f32[16,128,128]{2,1,0:T(8,128)}), f32[16,128,128]{2,1,0:T(8,128)}) %all-reduce.6.cloned.1.call-update) | async-done | bytes 1048592 | tf_op jit(solution)/shard_map/psum | solution.py:124
  176.3 4.4 %fusion.13 = bf16[16,128,512]{2,1,0:T(8,128)(2,1)} fusion(f32[16,128,128]{2,1,0:T(8,128)} %all-reduce.6.cloned.1.call-done, bf16[512,2048]{1,0:T(8,128)(2,1)S(1)} %copy-done), kind=kOutput, calls=%fused_computation.34 | convolution fusion | flops 1611661312 | bytes 5242880 | tf_op jit(solution)/shard_map/thd,hde->the/dot_general | solution.py:130
  180.8 4.0 %copy.84 = bf16[512,2048]{1,0:T(8,128)(2,1)} copy(bf16[512,2048]{0,1:T(8,128)(2,1)} %bitcast.155) | data formatting | bytes 4194304
  184.8 4.8 %fusion.16 = bf16[16,128,512]{2,1,0:T(8,128)(2,1)} fusion(f32[16,128,128]{2,1,0:T(8,128)S(1)} %copy-done.31, bf16[512,2048]{1,0:T(8,128)(2,1)} %param.13), kind=kOutput, calls=%fused_computation.35 | convolution fusion | flops 1611661312 | bytes 5242880 | tf_op jit(solution)/shard_map/the,hde->thd/dot_general | solution.py:127
  189.6 3.9 %copy.83 = bf16[512,2048]{1,0:T(8,128)(2,1)} copy(bf16[512,2048]{0,1:T(8,128)(2,1)} %bitcast.154) | data formatting | bytes 4194304
  (104 shorter events, 39.6 us)
Async XLA Ops:
  7.2 67.2 %all-reduce.4.cloned.1.call-start = ((), (), s32[]{:S(2)}) async-start(), calls=%async_computation | async-start | bytes 2097152 | tf_op jit(solution)/shard_map/psum | solution.py:17
  12.2 164.1 %all-reduce.6.cloned.1.call-start = ((), (), s32[]{:S(2)}) async-start(), calls=%async_computation.1 | async-start | bytes 2097152 | tf_op jit(solution)/shard_map/psum | solution.py:124
  28.2 4.8 %copy-start.20 = (bf16[256,2048]{0,1:T(8,128)(2,1)}, bf16[256,2048]{0,1:T(8,128)(2,1)S(1)}, u32[]{:S(2)}) copy-start(bf16[256,2048]{0,1:T(8,128)(2,1)S(1)} %get-tuple-element.31) | copy-start | bytes 3145732
  29.5 3.5 %copy-start.9 = (bf16[256,2048]{0,1:T(8,128)(2,1)}, bf16[256,2048]{0,1:T(8,128)(2,1)S(1)}, u32[]{:S(2)}) copy-start(bf16[256,2048]{0,1:T(8,128)(2,1)S(1)} %get-tuple-element.27) | copy-start | bytes 3145732
  30.5 2.5 %copy-start.16 = (bf16[16,256,256]{2,1,0:T(8,128)(2,1)}, bf16[16,256,256]{2,1,0:T(8,128)(2,1)S(1)}, u32[]{:S(2)}) copy-start(bf16[16,256,256]{2,1,0:T(8,128)(2,1)S(1)} %multiply_convert_fusion.3) | copy-start | bytes 6291460
  74.4 2.1 %copy-start.10 = (bf16[256,2048]{0,1:T(8,128)(2,1)S(1)}, bf16[256,2048]{0,1:T(8,128)(2,1)}, u32[]{:S(2)}) copy-start(bf16[256,2048]{0,1:T(8,128)(2,1)} %copy-done.9) | copy-start | bytes 3145732
  74.4 2.5 %copy-start.28 = (f32[16,128,256]{2,1,0:T(8,128)S(1)}, f32[16,128,256]{2,1,0:T(8,128)}, u32[]{:S(2)}) copy-start(f32[16,128,256]{2,1,0:T(8,128)} %fusion.46) | copy-start | bytes 6291460
  77.0 2.4 %copy-start.25 = (f32[16,128,256]{2,1,0:T(8,128)S(1)}, f32[16,128,256]{2,1,0:T(8,128)}, u32[]{:S(2)}) copy-start(f32[16,128,256]{2,1,0:T(8,128)} %fusion.45) | copy-start | bytes 6291460
  80.4 2.0 copy-start.1
  96.8 2.3 %copy-start.18 = (bf16[16,256,256]{2,1,0:T(8,128)(2,1)S(1)}, bf16[16,256,256]{2,1,0:T(8,128)(2,1)}, u32[]{:S(2)}) copy-start(bf16[16,256,256]{2,1,0:T(8,128)(2,1)} %multiply_convert_fusion.2) | copy-start | bytes 6291460
  96.9 3.9 %copy-start.7 = (bf16[256,2048]{0,1:T(8,128)(2,1)}, bf16[256,2048]{0,1:T(8,128)(2,1)S(1)}, u32[]{:S(2)}) copy-start(bf16[256,2048]{0,1:T(8,128)(2,1)S(1)} %get-tuple-element.25) | copy-start | bytes 3145732
  97.0 17.7 %copy-start.5 = (bf16[256,2048]{0,1:T(8,128)(2,1)}, bf16[256,2048]{0,1:T(8,128)(2,1)S(1)}, u32[]{:S(2)}) copy-start(bf16[256,2048]{0,1:T(8,128)(2,1)S(1)} %get-tuple-element.24) | copy-start | bytes 3145732
  101.6 13.1 %copy-start.19 = (f32[16,128,128]{2,1,0:T(8,128)}, f32[16,128,128]{2,1,0:T(8,128)S(1)}, u32[]{:S(2)}) copy-start(f32[16,128,128]{2,1,0:T(8,128)S(1)} %fusion.49) | copy-start | bytes 3145732
  102.4 1.8 copy-start.21
  104.2 2.1 %copy-start.17 = (bf16[16,256,256]{2,1,0:T(8,128)(2,1)S(1)}, bf16[16,256,256]{2,1,0:T(8,128)(2,1)}, u32[]{:S(2)}) copy-start(bf16[16,256,256]{2,1,0:T(8,128)(2,1)} %copy-done.16) | copy-start | bytes 6291460
  106.3 1.8 copy-start.3
  119.5 3.6 %copy-start.8 = (bf16[256,2048]{0,1:T(8,128)(2,1)S(1)}, bf16[256,2048]{0,1:T(8,128)(2,1)}, u32[]{:S(2)}) copy-start(bf16[256,2048]{0,1:T(8,128)(2,1)} %copy-done.7) | copy-start | bytes 3145732
  119.5 3.6 %copy-start.26 = (f32[16,128,256]{2,1,0:T(8,128)S(1)}, f32[16,128,256]{2,1,0:T(8,128)}, u32[]{:S(2)}) copy-start(f32[16,128,256]{2,1,0:T(8,128)} %fusion.48) | copy-start | bytes 6291460
  119.5 3.6 %copy-start.30 = (bf16[16,128,128]{2,1,0:T(8,128)(2,1)S(1)}, bf16[16,128,128]{2,1,0:T(8,128)(2,1)}, u32[]{:S(2)}) copy-start(bf16[16,128,128]{2,1,0:T(8,128)(2,1)} %copy-done.29) | copy-start | bytes 1572868
  124.7 2.3 %copy-start.24 = (f32[16,128,128]{2,1,0:T(8,128)S(1)}, f32[16,128,128]{2,1,0:T(8,128)}, u32[]{:S(2)}) copy-start(f32[16,128,128]{2,1,0:T(8,128)} %all-reduce.4.cloned.1.call-done) | copy-start | bytes 3145732
  124.7 3.0 %copy-start.27 = (f32[16,128,256]{2,1,0:T(8,128)S(1)}, f32[16,128,256]{2,1,0:T(8,128)}, u32[]{:S(2)}) copy-start(f32[16,128,256]{2,1,0:T(8,128)} %fusion.47) | copy-start | bytes 6291460
  133.6 4.0 %copy-start.4 = (bf16[256,2048]{0,1:T(8,128)(2,1)S(1)}, bf16[256,2048]{0,1:T(8,128)(2,1)}, u32[]{:S(2)}) copy-start(bf16[256,2048]{0,1:T(8,128)(2,1)} %copy-done.2) | copy-start | bytes 3145732
  137.6 2.4 %copy-start.33 = (bf16[256,16,128]{0,2,1:T(8,128)(2,1)S(1)}, bf16[256,16,128]{0,2,1:T(8,128)(2,1)}, u32[]{:S(2)}) copy-start(bf16[256,16,128]{0,2,1:T(8,128)(2,1)} %fusion.26) | copy-start | bytes 3145732
  180.8 4.0 %copy-start.31 = (f32[16,128,128]{2,1,0:T(8,128)S(1)}, f32[16,128,128]{2,1,0:T(8,128)}, u32[]{:S(2)}) copy-start(f32[16,128,128]{2,1,0:T(8,128)} %all-reduce.6.cloned.1.call-done) | copy-start | bytes 3145732
  (14 other events, 19.3 us)
Sparse Core Ops, SparseCore 0:
  12.3 62.0 all-reduce.3
  119.6 56.6 all-reduce.5
where the time goes:
time: 201 us; the launch traced here: 200 us
  waiting for transfers between devices  58.3 us (29%)
  local copies, waits for them, and re-layouts  53.5 us (27%)
  matrix products  49.9 us (25%)
  between operations  15 us (7%)
  other arithmetic  13.6 us (7%)
  blocking collectives  9.93 us (5%)
    unnamed x82, local copies, waits for them, and re-layouts  51.9 us
    psum x1, waiting for transfers between devices, summed_prefix(): return lax.psum(partial_state, 'seq')  31.3 us
    psum x1, waiting for transfers between devices, body(): total_grad = lax.psum(grad_state, 'seq')  27 us
    psum x1, blocking collectives, body(): lax.psum((jnp.sum(attended * attended, axis=1), jnp.sum(scaled_cot * atte...  9.93 us
    dot_general x2, matrix products, intra_block(): jnp.einsum('hbs,she->bhe', scores, v_block, preferred_element_type=jnp.fl...  6.21 us
    dot_general x2, matrix products, backward_block(): jnp.einsum('bhe,hde->bhd', v_block, grad_bf, preferred_element_type=jnp.f...  5.98 us
    dot_general x1, matrix products, body(): jnp.einsum('the,hde->thd', wide_values, total_grad, precision=lax.Precisi...  4.79 us
    dot_general x2, matrix products, backward_block(): jnp.einsum('bhd,hde->bhe', k_block, grad_bf, preferred_element_type=jnp.f...  4.79 us
  transfers between devices with their start and end apart: 2, of which 2 were waited for; matrix products, arithmetic and copies ran while one was open for 28% of the time, Pallas kernels for 0%

commit v1 on v0

v1 whole, which is shorter than its diff:
```python
import functools

import jax
import jax.numpy as jnp
from jax import lax
from jax.experimental import pallas as pl
from jax.experimental.pallas import tpu as pltpu
from jax.sharding import PartitionSpec as P

HEAD_DIM = 128
BLOCK = 256
EPS = 1e-06
MESH = pl.DeviceIdType.MESH
F32 = jnp.float32
BF16 = jnp.bfloat16
LEAD = 2
SKEW = 2


def mm(a, b, ca, cb):
    return lax.dot_general(a, b, (((ca,), (cb,)), ((), ())), preferred_element_type=F32)


def kernel(nh, ns, width, *refs):
    (q_hbm, k_hbm, v_hbm, dy_hbm, pk_hbm, pv_hbm, gain_ref, len_ref) = refs[:8]
    outs = refs[8:14]
    (q, k, v, dy, pk, pv, do, o, sc, mask, kv, mb, gb, sq, inn, rinv, coef) = refs[14:31]
    stage = refs[31:37]
    st_out, st_in = refs[37:39]
    bufs = (refs[39:46], refs[46:53])
    in_sem, out_sem, st_send, st_recv, send_sem, recv_sem = refs[53:59]

    rows, cols = q.shape
    heads = cols // HEAD_DIM
    nown = heads // 2
    nb = rows // BLOCK
    nz = ns // 2
    me_h = lax.axis_index("head")
    me_s = lax.axis_index("seq")
    z = me_s // 2
    core = me_s % 2
    own0 = core * nown
    oth0 = (1 - core) * nown
    partner = (me_h, z * 2 + 1 - core)
    right = (me_h, jnp.minimum(me_s + 2, ns - 1))
    left = (me_h, jnp.maximum(me_s - 2, 0))
    not_first = z > 0
    not_last = z < nz - 1

    def cs(h):
        return pl.ds(pl.multiple_of(h * HEAD_DIM, HEAD_DIM), HEAD_DIM)

    half = nown * HEAD_DIM

    def load_half(j, src, dst, first):
        c = pl.ds(pl.multiple_of(first * HEAD_DIM, HEAD_DIM), half)
        return pltpu.make_async_copy(src.at[:, c], dst.at[:, c], in_sem.at[j])

    loads = [
        load_half(0, pk_hbm, pk, oth0),
        load_half(1, pv_hbm, pv, oth0),
        load_half(2, pk_hbm, pk, own0),
        load_half(3, pv_hbm, pv, own0),
        pltpu.make_async_copy(q_hbm, q, in_sem.at[4]),
        pltpu.make_async_copy(k_hbm, k, in_sem.at[5]),
        pltpu.make_async_copy(v_hbm, v, in_sem.at[6]),
        pltpu.make_async_copy(dy_hbm, dy, in_sem.at[7]),
    ]
    for c in loads:
        c.start()

    barrier = pltpu.get_barrier_semaphore()
    pl.semaphore_signal(barrier, inc=1, device_id=partner, device_id_type=MESH)

    @pl.when(not_first)
    def _():
        pl.semaphore_signal(barrier, inc=1, device_id=left, device_id_type=MESH)

    @pl.when(not_last)
    def _():
        pl.semaphore_signal(barrier, inc=1, device_id=right, device_id_type=MESH)

    for d in range(1, nh):
        pl.semaphore_signal(
            barrier, inc=1, device_id=((me_h + d) % nh, me_s), device_id_type=MESH
        )

    live = lax.broadcasted_iota(jnp.int32, (rows, HEAD_DIM), 0) < len_ref[0]
    mask[...] = jnp.where(live, 1.0, 0.0).astype(BF16)
    sq[...] = jnp.zeros_like(sq)
    inn[...] = jnp.zeros_like(inn)
    pl.semaphore_wait(
        barrier, nh + not_first.astype(jnp.int32) + not_last.astype(jnp.int32)
    )
    for c in loads[:4]:
        c.wait()

    def causal():
        r = lax.broadcasted_iota(jnp.int32, (BLOCK, BLOCK), 0)
        c = lax.broadcasted_iota(jnp.int32, (BLOCK, BLOCK), 1)
        return r >= c

    def exchange(ph, produce, compute, consume):
        xo, xi, x, rin, rout, lin, lout_t = bufs[ph][:7]
        lout = lout_t.at[0]
        tot = lout_t.at[1]
        tin = lout_t.at[2]

        def hop(kind, src, dst, i, dev):
            return pltpu.make_async_remote_copy(
                src_ref=src.at[i],
                dst_ref=dst.at[i],
                send_sem=send_sem.at[ph, kind, i],
                recv_sem=recv_sem.at[ph, kind, i],
                device_id=dev,
                device_id_type=MESH,
            )

        def to_partner(i):
            return hop(0, xo, xi, i, partner)

        def to_right(i):
            return hop(1, rout, rin, i, right)

        def to_left(i):
            return hop(2, lout, lin, i, left)

        def total_out(i):
            return hop(3, tot, tin, i, partner)

        def give(i):
            xo[i] = produce(oth0 + i)
            to_partner(i).start()

        def first(i, carry):
            give(i)
            return carry

        lax.fori_loop(0, LEAD, first, 0)
        far = jnp.maximum(z, nz - 1 - z)
        late = max(SKEW * (nz - 1) + SKEW, nown)
        slots = max(heads, nown + late)

        def slot(s, carry):
            @pl.when(s + LEAD < nown)
            def _():
                give(s + LEAD)

            @pl.when(s < nown)
            def _():
                mine = produce(own0 + s)
                to_partner(s).wait_recv()
                x[s] = mine + xi[s]

            i_r = s - SKEW * z

            @pl.when((i_r >= 0) & (i_r < nown))
            def _():
                @pl.when(not_first)
                def _():
                    to_right(i_r).wait_recv()
                    rout[i_r] = rin[i_r] + x[i_r]

                @pl.when(jnp.logical_not(not_first))
                def _():
                    rout[i_r] = x[i_r]

                @pl.when(not_last)
                def _():
                    to_right(i_r).start()

            i_l = s - SKEW * (nz - 1 - z)

            @pl.when((i_l >= 0) & (i_l < nown))
            def _():
                @pl.when(not_last)
                def _():
                    to_left(i_l).wait_recv()
                    lout[i_l] = lin[i_l] + x[i_l]

                @pl.when(jnp.logical_not(not_last))
                def _():
                    lout[i_l] = x[i_l]

                @pl.when(not_first)
                def _():
                    to_left(i_l).start()

            i_t = s - SKEW * far

            @pl.when((i_t >= 0) & (i_t < nown))
            def _():
                @pl.when(not_last)
                def _():
                    tot[i_t] = rout[i_t] + lin[i_t]

                @pl.when(jnp.logical_not(not_last))
                def _():
                    tot[i_t] = rout[i_t]

                total_out(i_t).start()

            @pl.when(s < heads)
            def _():
                compute((own0 + s) % heads)

            @pl.when((i_t >= 0) & (i_t < nown))
            def _():
                consume(own0 + i_t, tot[i_t])

            i_o = s - late

            @pl.when((i_o >= 0) & (i_o < nown))
            def _():
                total_out(i_o).wait_recv()
                consume(oth0 + i_o, tin[i_o])

            return carry

        lax.fori_loop(0, slots, slot, 0)

        def drain(i, carry):
            to_partner(i).wait_send()
            total_out(i).wait_send()

            @pl.when(not_last)
            def _():
                to_right(i).wait_send()

            @pl.when(not_first)
            def _():
                to_left(i).wait_send()

            return carry

        lax.fori_loop(0, nown, drain, 0)

    def blk(ref, c, h):
        return ref[pl.ds(c * BLOCK, BLOCK), cs(h)]

    def prefix_part(h):
        return mm(pk[:, cs(h)], pv[:, cs(h)], 0, 0)

    def intra(h):
        m = mask[...]
        q[:, cs(h)] = q[:, cs(h)] * m
        k[:, cs(h)] = k[:, cs(h)] * m
        v[:, cs(h)] = v[:, cs(h)] * m
        run = None
        for c in range(nb):
            kc, vc = blk(k, c, h), blk(v, c, h)
            a = jnp.where(causal(), mm(blk(q, c, h), kc, 1, 1), 0.0).astype(BF16)
            sc[h, c] = a
            o[pl.ds(c * BLOCK, BLOCK), cs(h)] = mm(a, vc, 1, 0)
            if c < nb - 1:
                add = mm(kc, vc, 0, 0)
                run = add if run is None else run + add
                kv[h, c] = run

    def first_intra(h):
        intra(h)

    def use_state(h, state):
        g = gain_ref[:, cs(h)]
        for c in range(nb):
            st = (state if c == 0 else state + kv[h, c - 1]).astype(BF16)
            mb[h, c] = st
            r = pl.ds(c * BLOCK, BLOCK)
            oc = o[r, cs(h)] + mm(blk(q, c, h), st, 1, 0)
            o[r, cs(h)] = oc
            dm = blk(dy, c, h) * mask[r, :]
            dy[r, cs(h)] = dm
            sq[r, :] += oc * oc
            inn[r, :] += dm.astype(F32) * g * oc

    for c in loads[4:]:
        c.wait()
    exchange(0, prefix_part, first_intra, use_state)

    row_sq = jnp.sum(sq[...].T, axis=0, keepdims=True)
    row_in = jnp.sum(inn[...].T, axis=0, keepdims=True)
    st_out[...] = jnp.concatenate(
        [jnp.broadcast_to(row_sq, (4, rows)), jnp.broadcast_to(row_in, (4, rows))], axis=0
    )
    copies = []
    for d in range(1, nh):
        copies.append(
            pltpu.make_async_remote_copy(
                src_ref=st_out,
                dst_ref=st_in.at[d - 1],
                send_sem=st_send.at[d - 1],
                recv_sem=st_recv.at[d - 1],
                device_id=((me_h + d) % nh, me_s),
                device_id_type=MESH,
            )
        )
        copies[-1].start()
    total = st_out[...]
    for d in range(1, nh):
        copies[d - 1].wait_recv()
        total = total + st_in[d - 1]
    inv = 1.0 / jnp.sqrt(total[0:1] / width + EPS)
    cf = total[4:5] * (inv * inv * inv) / width
    rinv[...] = jnp.broadcast_to(inv, (HEAD_DIM, rows)).T
    coef[...] = jnp.broadcast_to(cf, (HEAD_DIM, rows)).T

    def put(j, h):
        pltpu.make_async_copy(
            stage[j].at[:, cs(h)], outs[j].at[:, cs(h)], out_sem.at[j]
        ).start()

    def state_grad(h):
        g = gain_ref[:, cs(h)]
        run = None
        for c in reversed(range(nb)):
            r = pl.ds(c * BLOCK, BLOCK)
            oc = o[r, cs(h)]
            ri = rinv[r, :]
            stage[0][r, cs(h)] = (g * oc * ri).astype(BF16)
            d = (blk(dy, c, h).astype(F32) * g * ri - oc * coef[r, :]).astype(BF16)
            do[r, cs(h)] = d
            if c < nb - 1:
                gb[h, c] = run.astype(BF16)
            part = mm(blk(q, c, h), d, 0, 0)
            run = part if run is None else run + part
        put(0, h)
        return run

    def grads(h):
        for c in range(nb):
            r = pl.ds(c * BLOCK, BLOCK)
            qc, kc, vc, dc = blk(q, c, h), blk(k, c, h), blk(v, c, h), blk(do, c, h)
            a = sc[h, c]
            p = jnp.where(causal(), mm(dc, vc, 1, 1), 0.0).astype(BF16)
            stage[1][r, cs(h)] = (mm(dc, mb[h, c], 1, 1) + mm(p, kc, 1, 0)).astype(BF16)
            kg = mm(p, qc, 0, 0)
            vg = mm(a, dc, 0, 0)
            if c < nb - 1:
                g = gb[h, c]
                kg = kg + mm(vc, g, 1, 1)
                vg = vg + mm(kc, g, 1, 0)
            stage[2][r, cs(h)] = kg.astype(BF16)
            stage[3][r, cs(h)] = vg.astype(BF16)
        put(1, h)
        put(2, h)
        put(3, h)

    def prefix_grads(h, state):
        hi = state.astype(BF16)
        lo = (state - hi.astype(F32)).astype(BF16)
        vals = pv[:, cs(h)]
        keys = pk[:, cs(h)]
        vv = jnp.concatenate([vals, vals], axis=1)
        kk = jnp.concatenate([keys, keys], axis=1)
        stage[4][:, cs(h)] = mm(vv, jnp.concatenate([hi, lo], axis=1), 1, 1).astype(BF16)
        stage[5][:, cs(h)] = mm(kk, jnp.concatenate([hi, lo], axis=0), 1, 0).astype(BF16)
        put(4, h)
        put(5, h)

    exchange(1, state_grad, grads, prefix_grads)
    for c in copies:
        c.wait_send()
    for j in range(6):
        pltpu.make_async_copy(stage[j], outs[j], out_sem.at[j]).wait()


def body(nh, ns, queries, keys, values, cotangent, prefix_keys, prefix_values, gain, lengths):
    rows, cols = queries.shape
    heads = cols // HEAD_DIM
    nown = heads // 2
    nb = rows // BLOCK
    any_spec = pl.BlockSpec(memory_space=pl.ANY)
    big = pltpu.VMEM((rows, cols), BF16)
    row = pltpu.VMEM((rows, HEAD_DIM), F32)
    st = pltpu.VMEM((nown, HEAD_DIM, HEAD_DIM), F32)
    states = [st, st, st, st, st, st, pltpu.VMEM((3, nown, HEAD_DIM, HEAD_DIM), F32)]
    scratch = (
        [big] * 7
        + [
            pltpu.VMEM((rows, cols), F32),
            pltpu.VMEM((heads, nb, BLOCK, BLOCK), BF16),
            pltpu.VMEM((rows, HEAD_DIM), BF16),
            pltpu.VMEM((heads, max(nb - 1, 1), HEAD_DIM, HEAD_DIM), F32),
            pltpu.VMEM((heads, nb, HEAD_DIM, HEAD_DIM), BF16),
            pltpu.VMEM((heads, max(nb - 1, 1), HEAD_DIM, HEAD_DIM), BF16),
            row,
            row,
            row,
            row,
        ]
        + [big] * 6
        + [pltpu.VMEM((8, rows), F32), pltpu.VMEM((max(nh - 1, 1), 8, rows), F32)]
        + states
        + states
        + [
            pltpu.SemaphoreType.DMA((8,)),
            pltpu.SemaphoreType.DMA((6,)),
            pltpu.SemaphoreType.DMA((max(nh - 1, 1),)),
            pltpu.SemaphoreType.DMA((max(nh - 1, 1),)),
            pltpu.SemaphoreType.DMA((2, 4, nown)),
            pltpu.SemaphoreType.DMA((2, 4, nown)),
        ]
    )
    out = jax.ShapeDtypeStruct((rows, cols), BF16)
    return tuple(
        pl.pallas_call(
            functools.partial(kernel, nh, ns, float(cols * nh)),
            out_shape=[out] * 6,
            in_specs=[any_spec] * 6
            + [
                pl.BlockSpec(memory_space=pltpu.VMEM),
                pl.BlockSpec(memory_space=pltpu.SMEM),
            ],
            out_specs=[any_spec] * 6,
            scratch_shapes=scratch,
            compiler_params=pltpu.CompilerParams(
                collective_id=0, has_side_effects=True, vmem_limit_bytes=60 * 1024 * 1024
            ),
        )(
            queries,
            keys,
            values,
            cotangent,
            prefix_keys,
            prefix_values,
            gain.reshape(1, cols),
            lengths,
        )
    )


def solution(mesh):
    nh, ns = mesh.shape["head"], mesh.shape["seq"]
    tok = P("seq", "head")
    return jax.shard_map(
        functools.partial(body, nh, ns),
        mesh=mesh,
        in_specs=(tok,) * 6 + (P("head"), P("seq")),
        out_specs=(tok,) * 6,
        check_vma=False,
    )
```

time: 201 us -> 84.5 us (0.42)
  Pallas kernels: 0 us -> 68.9 us
  waiting for transfers between devices: 58.3 us -> 0 us
  matrix products: 49.9 us -> 0 us
  local copies, waits for them, and re-layouts: 53.5 us -> 14 us
  between operations: 15 us -> 1.3 us
  other arithmetic: 13.6 us -> 0 us
  blocking collectives: 9.93 us -> 0 us
    pallas_call x0 -> x1, Pallas kernels: none -> 68.9 us  [body(): pl.pallas_call(functools.partial(kernel, nh, ns, float(cols * nh)), out_s...]
    psum x2 -> x0, waiting for transfers between devices: 58.3 us -> none  [the longest x1 31.3 us: summed_prefix(): return lax.psum(partial_state, 'seq')]
    dot_general x26 -> x0, matrix products: 49.9 us -> none  [the longest x2 6.21 us: intra_block(): jnp.einsum('hbs,she->bhe', scores, v_block, preferred_element_type=jnp.fl...]
    unnamed x82 -> x16, local copies, waits for them, and re-layouts: 51.9 us -> 14 us
    psum x1 -> x0, blocking collectives: 9.93 us -> none  [body(): lax.psum((jnp.sum(attended * attended, axis=1), jnp.sum(scaled_cot * atte...]
    concatenate x3 -> x0, other arithmetic: 4.53 us -> none  [the longest x1 1.51 us: body(): jnp.concatenate(query_parts, axis=0).reshape(tok_rows, tok_cols)]
    convert_element_type x3 -> x0, other arithmetic: 4.5 us -> none  [the longest x1 4.48 us: body(): out_grad = out_grad.astype(jnp.bfloat16).reshape(block_shape)]
    mul x2 -> x0, other arithmetic: 3.3 us -> none  [the longest x1 3.28 us: body(): k_live = (keys * live_mask).reshape(block_shape)]
  transfers between devices with their start and end apart: 2 -> 0, of which waited for: 2 -> 0; matrix products, arithmetic and copies ran while one was open for 28% -> 0% of each run, Pallas kernels for 0% -> 0%
where the time goes in v1:
time: 84.5 us; the launch traced here: 84.2 us
  Pallas kernels  68.9 us (82%)
  local copies, waits for them, and re-layouts  14 us (17%)
  between operations  1.3 us (2%)
    pallas_call x1, Pallas kernels, body(): pl.pallas_call(functools.partial(kernel, nh, ns, float(cols * nh)), out_s...  68.9 us
    unnamed x16, local copies, waits for them, and re-layouts  14 us

profile of v1, /device:TPU:0, one launch (start us, length us, event | category | flops | bytes accessed | tf_op | source)
XLA Modules:
  0.0 84.2 jit_solution(9731076269911896647)
XLA Ops:
  1.3 68.9 %shard_map.127 = (bf16[512,2048]{1,0:T(8,128)(2,1)}, bf16[512,2048]{1,0:T(8,128)(2,1)}, bf16[512,2048]{1,0:T(8,128)(2,1)}, bf16[512,2048]{1,0:T(8,128)(2,1)}, bf...) custom-call(bf16[512,2048]{1,0:T(8,128)(2,1)} %refs_0_.1, bf16[512,2048]{1,0:T(8,128)(2,1)} %refs_1_.1, ...), custom_call_target="tpu_custom_call" | custom-call | tf_op jit(solution)/shard_map/pallas_call | solution.py:406
  70.2 0.0 copy-start.4
  70.2 3.3 %copy.21 = bf16[512,2048]{1,0:T(8,128)(2,1)} copy(bf16[512,2048]{1,0:T(8,128)(2,1)} %get-tuple-element.12) | data formatting | bytes 4194304
  73.5 0.0 copy-done.4
  73.5 0.0 copy-start.3
  73.5 1.3 %copy.22 = bf16[512,2048]{1,0:T(8,128)(2,1)} copy(bf16[512,2048]{1,0:T(8,128)(2,1)S(1)} %copy-done.4) | data formatting | bytes 4194304
  74.8 1.0 %copy-done.3 = bf16[512,2048]{1,0:T(8,128)(2,1)S(1)} copy-done((bf16[512,2048]{1,0:T(8,128)(2,1)S(1)}, bf16[512,2048]{1,0:T(8,128)(2,1)}, u32[]{:S(2)}) %copy-start.3) | copy-done | bytes 2097176
  75.8 0.0 copy-start.2
  75.8 1.3 %copy.23 = bf16[512,2048]{1,0:T(8,128)(2,1)} copy(bf16[512,2048]{1,0:T(8,128)(2,1)S(1)} %copy-done.3) | data formatting | bytes 4194304
  77.2 1.0 %copy-done.2 = bf16[512,2048]{1,0:T(8,128)(2,1)S(1)} copy-done((bf16[512,2048]{1,0:T(8,128)(2,1)S(1)}, bf16[512,2048]{1,0:T(8,128)(2,1)}, u32[]{:S(2)}) %copy-start.2) | copy-done | bytes 2097176
  78.2 0.0 copy-start.1
  78.2 1.3 %copy.24 = bf16[512,2048]{1,0:T(8,128)(2,1)} copy(bf16[512,2048]{1,0:T(8,128)(2,1)S(1)} %copy-done.2) | data formatting | bytes 4194304
  79.5 1.0 %copy-done.1 = bf16[512,2048]{1,0:T(8,128)(2,1)S(1)} copy-done((bf16[512,2048]{1,0:T(8,128)(2,1)S(1)}, bf16[512,2048]{1,0:T(8,128)(2,1)}, u32[]{:S(2)}) %copy-start.1) | copy-done | bytes 2097176
  80.5 0.0 copy-start
  80.5 1.3 %copy.25 = bf16[512,2048]{1,0:T(8,128)(2,1)} copy(bf16[512,2048]{1,0:T(8,128)(2,1)S(1)} %copy-done.1) | data formatting | bytes 4194304
  81.8 1.0 %copy-done = bf16[512,2048]{1,0:T(8,128)(2,1)S(1)} copy-done((bf16[512,2048]{1,0:T(8,128)(2,1)S(1)}, bf16[512,2048]{1,0:T(8,128)(2,1)}, u32[]{:S(2)}) %copy-start) | copy-done | bytes 2097176
  82.9 1.3 %copy.26 = bf16[512,2048]{1,0:T(8,128)(2,1)} copy(bf16[512,2048]{1,0:T(8,128)(2,1)S(1)} %copy-done) | data formatting | bytes 4194304
Async XLA Ops:
  70.2 3.3 %copy-start.4 = (bf16[512,2048]{1,0:T(8,128)(2,1)S(1)}, bf16[512,2048]{1,0:T(8,128)(2,1)}, u32[]{:S(2)}) copy-start(bf16[512,2048]{1,0:T(8,128)(2,1)} %get-tuple-element.13) | copy-start | bytes 6291460
  73.5 2.3 %copy-start.3 = (bf16[512,2048]{1,0:T(8,128)(2,1)S(1)}, bf16[512,2048]{1,0:T(8,128)(2,1)}, u32[]{:S(2)}) copy-start(bf16[512,2048]{1,0:T(8,128)(2,1)} %get-tuple-element.14) | copy-start | bytes 6291460
  75.8 2.3 %copy-start.2 = (bf16[512,2048]{1,0:T(8,128)(2,1)S(1)}, bf16[512,2048]{1,0:T(8,128)(2,1)}, u32[]{:S(2)}) copy-start(bf16[512,2048]{1,0:T(8,128)(2,1)} %get-tuple-element.15) | copy-start | bytes 6291460
  78.2 2.3 %copy-start.1 = (bf16[512,2048]{1,0:T(8,128)(2,1)S(1)}, bf16[512,2048]{1,0:T(8,128)(2,1)}, u32[]{:S(2)}) copy-start(bf16[512,2048]{1,0:T(8,128)(2,1)} %get-tuple-element.16) | copy-start | bytes 6291460
  80.5 2.3 %copy-start = (bf16[512,2048]{1,0:T(8,128)(2,1)S(1)}, bf16[512,2048]{1,0:T(8,128)(2,1)}, u32[]{:S(2)}) copy-start(bf16[512,2048]{1,0:T(8,128)(2,1)} %get-tuple-element.17) | copy-start | bytes 6291460

commit v2 on v1

--- a/solution.py
+++ b/solution.py
@@ -23,12 +23,12 @@
 
 def kernel(nh, ns, width, *refs):
     (q_hbm, k_hbm, v_hbm, dy_hbm, pk_hbm, pv_hbm, gain_ref, len_ref) = refs[:8]
-    outs = refs[8:14]
-    (q, k, v, dy, pk, pv, do, o, sc, mask, kv, mb, gb, sq, inn, rinv, coef) = refs[14:31]
-    stage = refs[31:37]
-    st_out, st_in = refs[37:39]
-    bufs = (refs[39:46], refs[46:53])
-    in_sem, out_sem, st_send, st_recv, send_sem, recv_sem = refs[53:59]
+    stage = refs[8:12]
+    pk, pv, tout = refs[12:15]
+    (q, k, v, dy, do, o, sc, mask, kv, mb, gb, sq, inn, rinv, coef) = refs[15:30]
+    st_out, st_in = refs[30:32]
+    bufs = (refs[32:39], refs[39:46])
+    in_sem, st_send, st_recv, send_sem, recv_sem = refs[46:51]
 
     rows, cols = q.shape
     heads = cols // HEAD_DIM
@@ -304,11 +304,6 @@
     rinv[...] = jnp.broadcast_to(inv, (HEAD_DIM, rows)).T
     coef[...] = jnp.broadcast_to(cf, (HEAD_DIM, rows)).T
 
-    def put(j, h):
-        pltpu.make_async_copy(
-            stage[j].at[:, cs(h)], outs[j].at[:, cs(h)], out_sem.at[j]
-        ).start()
-
     def state_grad(h):
         g = gain_ref[:, cs(h)]
         run = None
@@ -323,7 +318,6 @@
                 gb[h, c] = run.astype(BF16)
             part = mm(blk(q, c, h), d, 0, 0)
             run = part if run is None else run + part
-        put(0, h)
         return run
 
     def grads(h):
@@ -341,27 +335,43 @@
                 vg = vg + mm(kc, g, 1, 0)
             stage[2][r, cs(h)] = kg.astype(BF16)
             stage[3][r, cs(h)] = vg.astype(BF16)
-        put(1, h)
-        put(2, h)
-        put(3, h)
-
-    def prefix_grads(h, state):
+
+    def keep_total(h, state):
+        tout[h] = state
+
+    exchange(1, state_grad, grads, keep_total)
+    for c in copies:
+        c.wait_send()
+
+
+def finish(*refs):
+    ready = refs[:4]
+    pk, pv, total = refs[4:7]
+    outs = refs[7:13]
+    pkg, pvg, sem = refs[13:16]
+    heads = total.shape[0]
+    for j in range(4):
+        pltpu.make_async_copy(ready[j], outs[j], sem.at[j]).start()
+
+    def head(h, carry):
+        c = pl.ds(pl.multiple_of(h * HEAD_DIM, HEAD_DIM), HEAD_DIM)
+        state = total[h]
         hi = state.astype(BF16)
         lo = (state - hi.astype(F32)).astype(BF16)
-        vals = pv[:, cs(h)]
-        keys = pk[:, cs(h)]
+        vals, keys = pv[:, c], pk[:, c]
         vv = jnp.concatenate([vals, vals], axis=1)
         kk = jnp.concatenate([keys, keys], axis=1)
-        stage[4][:, cs(h)] = mm(vv, jnp.concatenate([hi, lo], axis=1), 1, 1).astype(BF16)
-        stage[5][:, cs(h)] = mm(kk, jnp.concatenate([hi, lo], axis=0), 1, 0).astype(BF16)
-        put(4, h)
-        put(5, h)
-
-    exchange(1, state_grad, grads, prefix_grads)
-    for c in copies:
-        c.wait_send()
-    for j in range(6):
-        pltpu.make_async_copy(stage[j], outs[j], out_sem.at[j]).wait()
+        pkg[:, c] = mm(vv, jnp.concatenate([hi, lo], axis=1), 1, 1).astype(BF16)
+        pvg[:, c] = mm(kk, jnp.concatenate([hi, lo], axis=0), 1, 0).astype(BF16)
+        pltpu.make_async_copy(pkg.at[:, c], outs[4].at[:, c], sem.at[4]).start()
+        pltpu.make_async_copy(pvg.at[:, c], outs[5].at[:, c], sem.at[5]).start()
+        return carry
+
+    lax.fori_loop(0, heads, head, 0)
+    for j in range(4):
+        pltpu.make_async_copy(ready[j], outs[j], sem.at[j]).wait()
+    pltpu.make_async_copy(pkg, outs[4], sem.at[4]).wait()
+    pltpu.make_async_copy(pvg, outs[5], sem.at[5]).wait()
 
 
 def body(nh, ns, queries, keys, values, cotangent, prefix_keys, prefix_values, gain, lengths):
@@ -375,7 +385,7 @@
     st = pltpu.VMEM((nown, HEAD_DIM, HEAD_DIM), F32)
     states = [st, st, st, st, st, st, pltpu.VMEM((3, nown, HEAD_DIM, HEAD_DIM), F32)]
     scratch = (
-        [big] * 7
+        [big] * 5
         + [
             pltpu.VMEM((rows, cols), F32),
             pltpu.VMEM((heads, nb, BLOCK, BLOCK), BF16),
@@ -388,44 +398,42 @@
             row,
             row,
         ]
-        + [big] * 6
         + [pltpu.VMEM((8, rows), F32), pltpu.VMEM((max(nh - 1, 1), 8, rows), F32)]
         + states
         + states
         + [
             pltpu.SemaphoreType.DMA((8,)),
-            pltpu.SemaphoreType.DMA((6,)),
             pltpu.SemaphoreType.DMA((max(nh - 1, 1),)),
             pltpu.SemaphoreType.DMA((max(nh - 1, 1),)),
             pltpu.SemaphoreType.DMA((2, 4, nown)),
             pltpu.SemaphoreType.DMA((2, 4, nown)),
         ]
     )
-    out = jax.ShapeDtypeStruct((rows, cols), BF16)
+    fast = pl.BlockSpec(memory_space=pltpu.VMEM)
+    tot = pltpu.VMEM((heads, HEAD_DIM, HEAD_DIM), F32)
+    wide = [queries, keys, values, cotangent, prefix_keys, prefix_values]
+    wide = [pltpu.with_memory_space_constraint(x, pltpu.HBM) for x in wide]
+    made = pl.pallas_call(
+        functools.partial(kernel, nh, ns, float(cols * nh)),
+        out_shape=[big] * 6 + [tot],
+        in_specs=[any_spec] * 6 + [fast, pl.BlockSpec(memory_space=pltpu.SMEM)],
+        out_specs=[fast] * 7,
+        scratch_shapes=scratch,
+        compiler_params=pltpu.CompilerParams(
+            collective_id=0, has_side_effects=True, vmem_limit_bytes=36 * 1024 * 1024
+        ),
+    )(*wide, gain.reshape(1, cols), lengths)
+    made = [pltpu.with_memory_space_constraint(x, pltpu.VMEM) for x in made]
+    out = pltpu.HBM((rows, cols), BF16)
     return tuple(
         pl.pallas_call(
-            functools.partial(kernel, nh, ns, float(cols * nh)),
+            finish,
             out_shape=[out] * 6,
-            in_specs=[any_spec] * 6
-            + [
-                pl.BlockSpec(memory_space=pltpu.VMEM),
-                pl.BlockSpec(memory_space=pltpu.SMEM),
-            ],
+            in_specs=[fast] * 7,
             out_specs=[any_spec] * 6,
-            scratch_shapes=scratch,
-            compiler_params=pltpu.CompilerParams(
-                collective_id=0, has_side_effects=True, vmem_limit_bytes=60 * 1024 * 1024
-            ),
-        )(
-            queries,
-            keys,
-            values,
-            cotangent,
-            prefix_keys,
-            prefix_values,
-            gain.reshape(1, cols),
-            lengths,
-        )
+            scratch_shapes=[big, big, pltpu.SemaphoreType.DMA((6,))],
+            compiler_params=pltpu.CompilerParams(vmem_limit_bytes=8 * 1024 * 1024),
+        )(*made)
     )
 
 

time: 84.5 us -> 73.5 us (0.87)
  local copies, waits for them, and re-layouts: 14 us -> 0.69 us
  Pallas kernels: 68.9 us -> 71.3 us
    unnamed x16 -> x2, local copies, waits for them, and re-layouts: 14 us -> 0.69 us
    pallas_call x0 -> x1, Pallas kernels: none -> 5.62 us  [body(): pl.pallas_call(finish, out_shape=[out] * 6, in_specs=[fast] * 7, out_spec...]
    pallas_call x1, Pallas kernels: 68.9 us -> 65.7 us  [body(): pl.pallas_call(functools.partial(kernel, nh, ns, float(cols * nh)), out_s...]
where the time goes in v2:
time: 73.5 us; the launch traced here: 73.3 us
  Pallas kernels  71.3 us (97%)
  between operations  1.3 us (2%)
    pallas_call x1, Pallas kernels, body(): pl.pallas_call(functools.partial(kernel, nh, ns, float(cols * nh)), out_s...  65.7 us
    pallas_call x1, Pallas kernels, body(): pl.pallas_call(finish, out_shape=[out] * 6, in_specs=[fast] * 7, out_spec...  5.62 us

profile of v2, /device:TPU:0, one launch (start us, length us, event | category | flops | bytes accessed | tf_op | source)
XLA Modules:
  0.0 73.3 jit_solution(2189913809893363872)
XLA Ops:
  1.3 0.0 copy-start
  1.3 0.7 copy-done
  2.0 65.7 %shard_map.127 = (bf16[512,2048]{1,0:T(8,128)(2,1)S(1)}, bf16[512,2048]{1,0:T(8,128)(2,1)S(1)}, bf16[512,2048]{1,0:T(8,128)(2,1)S(1)}, bf16[512,2048]{1,0:T(8,12...) custom-call(bf16[512,2048]{1,0:T(8,128)(2,1)} %refs_0_.1, ...), custom_call_target="tpu_custom_call" | custom-call | tf_op jit(solution)/shard_map/pallas_call | solution.py:416
  67.7 5.6 %shard_map.128 = (bf16[512,2048]{1,0:T(8,128)(2,1)}, bf16[512,2048]{1,0:T(8,128)(2,1)}, bf16[512,2048]{1,0:T(8,128)(2,1)}, bf16[512,2048]{1,0:T(8,128)(2,1)}, bf...) custom-call(bf16[512,2048]{1,0:T(8,128)(2,1)S(1)} %get-tuple-element.13.refs_0_, ...), custom_call_target="tpu_custom_call" | custom-call | tf_op jit(solution)/shard_map/pallas_call | solution.py:429
Async XLA Ops:
  1.3 0.7 copy-start

commit v3 on v2

--- a/solution.py
+++ b/solution.py
@@ -14,7 +14,8 @@
 F32 = jnp.float32
 BF16 = jnp.bfloat16
 LEAD = 2
-SKEW = 2
+SUB = 1
+SKEW = 3
 
 
 def mm(a, b, ca, cb):
@@ -22,13 +23,13 @@
 
 
 def kernel(nh, ns, width, *refs):
-    (q_hbm, k_hbm, v_hbm, dy_hbm, pk_hbm, pv_hbm, gain_ref, len_ref) = refs[:8]
+    (q_hbm, k_hbm, v_hbm, dy_hbm, pk_hbm, pv_hbm, gain_hbm, len_ref) = refs[:8]
     stage = refs[8:12]
     pk, pv, tout = refs[12:15]
     (q, k, v, dy, do, o, sc, mask, kv, mb, gb, sq, inn, rinv, coef) = refs[15:30]
     st_out, st_in = refs[30:32]
-    bufs = (refs[32:39], refs[39:46])
-    in_sem, st_send, st_recv, send_sem, recv_sem = refs[46:51]
+    bufs = (refs[32:41], refs[41:50])
+    in_sem, st_send, st_recv, send_sem, recv_sem, gain_ref = refs[50:56]
 
     rows, cols = q.shape
     heads = cols // HEAD_DIM
@@ -65,6 +66,7 @@
         pltpu.make_async_copy(k_hbm, k, in_sem.at[5]),
         pltpu.make_async_copy(v_hbm, v, in_sem.at[6]),
         pltpu.make_async_copy(dy_hbm, dy, in_sem.at[7]),
+        pltpu.make_async_copy(gain_hbm, gain_ref, in_sem.at[8]),
     ]
     for c in loads:
         c.start()
@@ -92,7 +94,7 @@
     pl.semaphore_wait(
         barrier, nh + not_first.astype(jnp.int32) + not_last.astype(jnp.int32)
     )
-    for c in loads[:4]:
+    for c in loads[:2]:
         c.wait()
 
     def causal():
@@ -100,16 +102,14 @@
         c = lax.broadcasted_iota(jnp.int32, (BLOCK, BLOCK), 1)
         return r >= c
 
-    def exchange(ph, produce, compute, consume):
-        xo, xi, x, rin, rout, lin, lout_t = bufs[ph][:7]
-        lout = lout_t.at[0]
-        tot = lout_t.at[1]
-        tin = lout_t.at[2]
+    def exchange(ph, produce, compute, consume, ready):
+        xo, xi, x, rin, rout, lin, lout, tot, tin = bufs[ph]
+        pieces = nown * SUB
 
         def hop(kind, src, dst, i, dev):
             return pltpu.make_async_remote_copy(
-                src_ref=src.at[i],
-                dst_ref=dst.at[i],
+                src_ref=src,
+                dst_ref=dst,
                 send_sem=send_sem.at[ph, kind, i],
                 recv_sem=recv_sem.at[ph, kind, i],
                 device_id=dev,
@@ -117,19 +117,22 @@
             )
 
         def to_partner(i):
-            return hop(0, xo, xi, i, partner)
+            return hop(0, xo.at[i], xi.at[i], i, partner)
+
+        def total_out(i):
+            return hop(1, tot.at[i], tin.at[i], i, partner)
 
         def to_right(i):
-            return hop(1, rout, rin, i, right)
+            return hop(2, rout.at[i // SUB, i % SUB], rin.at[i // SUB, i % SUB], i, right)
 
         def to_left(i):
-            return hop(2, lout, lin, i, left)
-
-        def total_out(i):
-            return hop(3, tot, tin, i, partner)
+            return hop(3, lout.at[i // SUB, i % SUB], lin.at[i // SUB, i % SUB], i, left)
+
+        def split(state):
+            return state.reshape(SUB, HEAD_DIM // SUB, HEAD_DIM)
 
         def give(i):
-            xo[i] = produce(oth0 + i)
+            xo[i] = split(produce(oth0 + i))
             to_partner(i).start()
 
         def first(i, carry):
@@ -137,9 +140,49 @@
             return carry
 
         lax.fori_loop(0, LEAD, first, 0)
+        ready(-1)
         far = jnp.maximum(z, nz - 1 - z)
-        late = max(SKEW * (nz - 1) + SKEW, nown)
+        late = max((SKEW * (nz - 1) + SUB - 1) // SUB + 2, nown)
         slots = max(heads, nown + late)
+
+        def step(t):
+            i_r = t - SKEW * z
+
+            @pl.when((i_r >= 0) & (i_r < pieces))
+            def _():
+                i, j = i_r // SUB, i_r % SUB
+
+                @pl.when(not_first)
+                def _():
+                    to_right(i_r).wait_recv()
+                    rout[i, j] = rin[i, j] + x[i, j]
+
+                @pl.when(jnp.logical_not(not_first))
+                def _():
+                    rout[i, j] = x[i, j]
+
+                @pl.when(not_last)
+                def _():
+                    to_right(i_r).start()
+
+            i_l = t - SKEW * (nz - 1 - z)
+
+            @pl.when((i_l >= 0) & (i_l < pieces))
+            def _():
+                i, j = i_l // SUB, i_l % SUB
+
+                @pl.when(not_last)
+                def _():
+                    to_left(i_l).wait_recv()
+                    lout[i, j] = lin[i, j] + x[i, j]
+
+                @pl.when(jnp.logical_not(not_last))
+                def _():
+                    lout[i, j] = x[i, j]
+
+                @pl.when(not_first)
+                def _():
+                    to_left(i_l).start()
 
         def slot(s, carry):
             @pl.when(s + LEAD < nown)
@@ -148,72 +191,41 @@
 
             @pl.when(s < nown)
             def _():
-                mine = produce(own0 + s)
+                mine = split(produce(own0 + s))
                 to_partner(s).wait_recv()
                 x[s] = mine + xi[s]
 
-            i_r = s - SKEW * z
-
-            @pl.when((i_r >= 0) & (i_r < nown))
-            def _():
-                @pl.when(not_first)
-                def _():
-                    to_right(i_r).wait_recv()
-                    rout[i_r] = rin[i_r] + x[i_r]
-
-                @pl.when(jnp.logical_not(not_first))
-                def _():
-                    rout[i_r] = x[i_r]
-
+            ready(s)
+            for j in range(SUB):
+                step(s * SUB + j)
+                if j == 0:
+
+                    @pl.when(s < heads)
+                    def _():
+                        for c in range(nb):
+                            compute((own0 + s) % heads, c)
+
+            i_t = s - (SKEW * far + SUB - 1) // SUB
+
+            @pl.when((i_t >= 0) & (i_t < nown))
+            def _():
                 @pl.when(not_last)
                 def _():
-                    to_right(i_r).start()
-
-            i_l = s - SKEW * (nz - 1 - z)
-
-            @pl.when((i_l >= 0) & (i_l < nown))
-            def _():
-                @pl.when(not_last)
-                def _():
-                    to_left(i_l).wait_recv()
-                    lout[i_l] = lin[i_l] + x[i_l]
+                    tot[i_t] = rout[i_t] + lin[i_t]
 
                 @pl.when(jnp.logical_not(not_last))
                 def _():
-                    lout[i_l] = x[i_l]
-
-                @pl.when(not_first)
-                def _():
-                    to_left(i_l).start()
-
-            i_t = s - SKEW * far
-
-            @pl.when((i_t >= 0) & (i_t < nown))
-            def _():
-                @pl.when(not_last)
-                def _():
-                    tot[i_t] = rout[i_t] + lin[i_t]
-
-                @pl.when(jnp.logical_not(not_last))
-                def _():
                     tot[i_t] = rout[i_t]
 
                 total_out(i_t).start()
-
-            @pl.when(s < heads)
-            def _():
-                compute((own0 + s) % heads)
-
-            @pl.when((i_t >= 0) & (i_t < nown))
-            def _():
-                consume(own0 + i_t, tot[i_t])
+                consume(own0 + i_t, tot[i_t].reshape(HEAD_DIM, HEAD_DIM))
 
             i_o = s - late
 
             @pl.when((i_o >= 0) & (i_o < nown))
             def _():
                 total_out(i_o).wait_recv()
-                consume(oth0 + i_o, tin[i_o])
+                consume(oth0 + i_o, tin[i_o].reshape(HEAD_DIM, HEAD_DIM))
 
             return carry
 
@@ -222,7 +234,11 @@
         def drain(i, carry):
             to_partner(i).wait_send()
             total_out(i).wait_send()
-
+            return carry
+
+        lax.fori_loop(0, nown, drain, 0)
+
+        def drain_hop(i, carry):
             @pl.when(not_last)
             def _():
                 to_right(i).wait_send()
@@ -233,7 +249,7 @@
 
             return carry
 
-        lax.fori_loop(0, nown, drain, 0)
+        lax.fori_loop(0, pieces, drain_hop, 0)
 
     def blk(ref, c, h):
         return ref[pl.ds(c * BLOCK, BLOCK), cs(h)]
@@ -241,24 +257,35 @@
     def prefix_part(h):
         return mm(pk[:, cs(h)], pv[:, cs(h)], 0, 0)
 
-    def intra(h):
-        m = mask[...]
-        q[:, cs(h)] = q[:, cs(h)] * m
-        k[:, cs(h)] = k[:, cs(h)] * m
-        v[:, cs(h)] = v[:, cs(h)] * m
-        run = None
-        for c in range(nb):
-            kc, vc = blk(k, c, h), blk(v, c, h)
-            a = jnp.where(causal(), mm(blk(q, c, h), kc, 1, 1), 0.0).astype(BF16)
-            sc[h, c] = a
-            o[pl.ds(c * BLOCK, BLOCK), cs(h)] = mm(a, vc, 1, 0)
-            if c < nb - 1:
-                add = mm(kc, vc, 0, 0)
-                run = add if run is None else run + add
-                kv[h, c] = run
-
-    def first_intra(h):
-        intra(h)
+    def intra(h, c):
+        r = pl.ds(c * BLOCK, BLOCK)
+        m = mask[r, :]
+        qc, kc, vc = blk(q, c, h) * m, blk(k, c, h) * m, blk(v, c, h) * m
+        q[r, cs(h)] = qc
+        k[r, cs(h)] = kc
+        v[r, cs(h)] = vc
+        a = jnp.where(causal(), mm(qc, kc, 1, 1), 0.0).astype(BF16)
+        sc[h, c] = a
+        o[r, cs(h)] = mm(a, vc, 1, 0)
+        if c < nb - 1:
+            add = mm(kc, vc, 0, 0)
+            kv[h, c] = add if c == 0 else kv[h, c - 1] + add
+
+    def loaded(s):
+        if isinstance(s, int):
+            for c in loads[2:4]:
+                c.wait()
+            return
+
+        @pl.when(s == 0)
+        def _():
+            for c in loads[4:7]:
+                c.wait()
+
+        @pl.when(s == 1)
+        def _():
+            loads[7].wait()
+            loads[8].wait()
 
     def use_state(h, state):
         g = gain_ref[:, cs(h)]
@@ -273,9 +300,7 @@
             sq[r, :] += oc * oc
             inn[r, :] += dm.astype(F32) * g * oc
 
-    for c in loads[4:]:
-        c.wait()
-    exchange(0, prefix_part, first_intra, use_state)
+    exchange(0, prefix_part, intra, use_state, loaded)
 
     row_sq = jnp.sum(sq[...].T, axis=0, keepdims=True)
     row_in = jnp.sum(inn[...].T, axis=0, keepdims=True)
@@ -320,26 +345,25 @@
             run = part if run is None else run + part
         return run
 
-    def grads(h):
-        for c in range(nb):
-            r = pl.ds(c * BLOCK, BLOCK)
-            qc, kc, vc, dc = blk(q, c, h), blk(k, c, h), blk(v, c, h), blk(do, c, h)
-            a = sc[h, c]
-            p = jnp.where(causal(), mm(dc, vc, 1, 1), 0.0).astype(BF16)
-            stage[1][r, cs(h)] = (mm(dc, mb[h, c], 1, 1) + mm(p, kc, 1, 0)).astype(BF16)
-            kg = mm(p, qc, 0, 0)
-            vg = mm(a, dc, 0, 0)
-            if c < nb - 1:
-                g = gb[h, c]
-                kg = kg + mm(vc, g, 1, 1)
-                vg = vg + mm(kc, g, 1, 0)
-            stage[2][r, cs(h)] = kg.astype(BF16)
-            stage[3][r, cs(h)] = vg.astype(BF16)
+    def grads(h, c):
+        r = pl.ds(c * BLOCK, BLOCK)
+        qc, kc, vc, dc = blk(q, c, h), blk(k, c, h), blk(v, c, h), blk(do, c, h)
+        a = sc[h, c]
+        p = jnp.where(causal(), mm(dc, vc, 1, 1), 0.0).astype(BF16)
+        stage[1][r, cs(h)] = (mm(dc, mb[h, c], 1, 1) + mm(p, kc, 1, 0)).astype(BF16)
+        kg = mm(p, qc, 0, 0)
+        vg = mm(a, dc, 0, 0)
+        if c < nb - 1:
+            g = gb[h, c]
+            kg = kg + mm(vc, g, 1, 1)
+            vg = vg + mm(kc, g, 1, 0)
+        stage[2][r, cs(h)] = kg.astype(BF16)
+        stage[3][r, cs(h)] = vg.astype(BF16)
 
     def keep_total(h, state):
         tout[h] = state
 
-    exchange(1, state_grad, grads, keep_total)
+    exchange(1, state_grad, grads, keep_total, lambda s: None)
     for c in copies:
         c.wait_send()
 
@@ -382,8 +406,7 @@
     any_spec = pl.BlockSpec(memory_space=pl.ANY)
     big = pltpu.VMEM((rows, cols), BF16)
     row = pltpu.VMEM((rows, HEAD_DIM), F32)
-    st = pltpu.VMEM((nown, HEAD_DIM, HEAD_DIM), F32)
-    states = [st, st, st, st, st, st, pltpu.VMEM((3, nown, HEAD_DIM, HEAD_DIM), F32)]
+    states = [pltpu.VMEM((nown, SUB, HEAD_DIM // SUB, HEAD_DIM), F32)] * 9
     scratch = (
         [big] * 5
         + [
@@ -402,27 +425,29 @@
         + states
         + states
         + [
-            pltpu.SemaphoreType.DMA((8,)),
+            pltpu.SemaphoreType.DMA((9,)),
             pltpu.SemaphoreType.DMA((max(nh - 1, 1),)),
             pltpu.SemaphoreType.DMA((max(nh - 1, 1),)),
-            pltpu.SemaphoreType.DMA((2, 4, nown)),
-            pltpu.SemaphoreType.DMA((2, 4, nown)),
+            pltpu.SemaphoreType.DMA((2, 4, nown * SUB)),
+            pltpu.SemaphoreType.DMA((2, 4, nown * SUB)),
+            pltpu.VMEM((1, cols), F32),
         ]
     )
     fast = pl.BlockSpec(memory_space=pltpu.VMEM)
     tot = pltpu.VMEM((heads, HEAD_DIM, HEAD_DIM), F32)
     wide = [queries, keys, values, cotangent, prefix_keys, prefix_values]
+    wide.append(gain.reshape(1, cols))
     wide = [pltpu.with_memory_space_constraint(x, pltpu.HBM) for x in wide]
     made = pl.pallas_call(
         functools.partial(kernel, nh, ns, float(cols * nh)),
         out_shape=[big] * 6 + [tot],
-        in_specs=[any_spec] * 6 + [fast, pl.BlockSpec(memory_space=pltpu.SMEM)],
+        in_specs=[any_spec] * 7 + [pl.BlockSpec(memory_space=pltpu.SMEM)],
         out_specs=[fast] * 7,
         scratch_shapes=scratch,
         compiler_params=pltpu.CompilerParams(
             collective_id=0, has_side_effects=True, vmem_limit_bytes=36 * 1024 * 1024
         ),
-    )(*wide, gain.reshape(1, cols), lengths)
+    )(*wide, lengths)
     made = [pltpu.with_memory_space_constraint(x, pltpu.VMEM) for x in made]
     out = pltpu.HBM((rows, cols), BF16)
     return tuple(

time: 73.5 us -> 65.5 us (0.89)
  Pallas kernels: 71.3 us -> 64.1 us
    pallas_call x1, Pallas kernels: 65.7 us -> 58.4 us  [body(): pl.pallas_call(functools.partial(kernel, nh, ns, float(cols * nh)), out_s...]
where the time goes in v3:
time: 65.5 us; the launch traced here: 65.3 us
  Pallas kernels  64.1 us (98%)
  between operations  1.29 us (2%)
    pallas_call x1, Pallas kernels, body(): pl.pallas_call(functools.partial(kernel, nh, ns, float(cols * nh)), out_s...  58.4 us
    pallas_call x1, Pallas kernels, body(): pl.pallas_call(finish, out_shape=[out] * 6, in_specs=[fast] * 7, out_spec...  5.62 us

profile of v3, /device:TPU:0, one launch (start us, length us, event | category | flops | bytes accessed | tf_op | source)
XLA Modules:
  0.0 65.3 jit_solution(16640650381762302524)
XLA Ops:
  1.3 58.4 %shard_map.127 = (bf16[512,2048]{1,0:T(8,128)(2,1)S(1)}, bf16[512,2048]{1,0:T(8,128)(2,1)S(1)}, bf16[512,2048]{1,0:T(8,128)(2,1)S(1)}, bf16[512,2048]{1,0:T(8,12...) custom-call(bf16[512,2048]{1,0:T(8,128)(2,1)} %refs_0_.1, ...), custom_call_target="tpu_custom_call" | custom-call | tf_op jit(solution)/shard_map/pallas_call | solution.py:441
  59.7 5.6 %shard_map.128 = (bf16[512,2048]{1,0:T(8,128)(2,1)}, bf16[512,2048]{1,0:T(8,128)(2,1)}, bf16[512,2048]{1,0:T(8,128)(2,1)}, bf16[512,2048]{1,0:T(8,128)(2,1)}, bf...) custom-call(bf16[512,2048]{1,0:T(8,128)(2,1)S(1)} %get-tuple-element.13.refs_0_, ...), custom_call_target="tpu_custom_call" | custom-call | tf_op jit(solution)/shard_map/pallas_call | solution.py:454
